TPU v7x, 256 devices: a whole 4x4x8 slice. The times are simulated.
256 devices in a mesh: seq: 32 (over z, x), dp: 8 (over y, core).
Axes of the slice: x: 4, y: 4, z: 8, core: 2. Of those that a mesh axis runs over, the one named last changes fastest.
Arguments:
- tokens: bfloat16 [8, 16384, 4096], P('dp', 'seq'), may hold values from -6 to 6
- w_in: bfloat16 [4096, 2336], P(('seq', 'dp')), may hold values from -0.09375 to 0.09375
- conv_w: float32 [4, 2304], replicated, may hold values from -3 to 3
- a_rate: float32 [32], replicated, may hold values from 3.0517579e-06 to 0.06
- d_skip: float32 [32], replicated, may hold values from 0.5 to 2
- level_w: int32 [8, 11], P('dp'), may hold values from 0 to 256
- lengths: int32 [8], P('dp'), may hold values from 64 to 16384, as said below
Outputs:
- mixed_out: bfloat16 [8, 16384, 2048], P('dp', 'seq')
Inputs may be any that keep to these rules, and one draw needn't show every extreme that they name: `lengths`: every length is a multiple of 64, and some request has all 16384 positions live.
All inputs are finite; a program needn't handle non-finite values.
Results may differ from a plain program's by a relative error of at most 0.015.
Values may be sent and summed in bfloat16 or wider, within the bound.
No kernel may reach another device: no remote copies, remote signals or barrier semaphores. Data moves between devices by JAX's collectives and lax.ppermute only.
A program may use at most 128 MiB of HBM per device.

v0:
```python
import jax
import jax.numpy as jnp
import numpy as np
from jax import lax
from jax.sharding import PartitionSpec as P

STATE = 128
Q = 64


def passed_along(array, axis, by):
    count = lax.axis_size(axis)
    pairs = [(i, i + by) for i in range(count) if 0 <= i + by < count]
    return lax.ppermute(array, axis, pairs)


def swapped(value, axis, stride):
    mask = 2**stride
    pairs = [(source, source ^ mask) for source in range(lax.axis_size(axis))]
    return lax.ppermute(value, axis, pairs)


def body(tokens, w_in, conv_w, a_rate, d_skip, level_w, lengths):
    token_rows = tokens.reshape(-1, tokens.shape[-1])
    count = token_rows.shape[0]
    projected = jnp.dot(
        token_rows,
        lax.all_gather(w_in, ("seq", "dp"), axis=0, tiled=True),
        preferred_element_type=jnp.float32,
    )
    kernel = conv_w.shape[0]
    channels = conv_w.shape[1]
    heads = a_rate.shape[0]
    inner = channels - 2 * STATE
    raw = projected[:, :channels].astype(jnp.bfloat16)
    rim = passed_along(raw[count - (kernel - 1) :], "seq", 1)
    padded = jnp.concatenate([rim, raw], 0)
    convolved = jnp.zeros((count, channels), jnp.float32)
    for offset in range(kernel):
        convolved = convolved + padded[offset : offset + count].astype(jnp.float32) * conv_w[offset]
    values = jax.nn.silu(convolved[:, :inner]).astype(jnp.bfloat16)
    in_b = convolved[:, inner : inner + STATE].astype(jnp.bfloat16)
    out_c = convolved[:, inner + STATE :].astype(jnp.bfloat16)
    step_size = jax.nn.softplus(projected[:, channels:])
    log_decay = -step_size * a_rate[None, :]
    head_dim = inner // heads
    driven = (
        values.astype(jnp.float32).reshape(count, heads, head_dim) * step_size[:, :, None]
    ).astype(jnp.bfloat16)
    stretches = count // Q
    cumul = jnp.cumsum(log_decay.reshape(stretches, Q, heads), axis=1)
    totals = cumul[:, -1]
    before = jnp.cumsum(totals, axis=0) - totals
    level_wt = level_w.reshape(-1).astype(jnp.float32) / 256.0
    keys_b = in_b.reshape(stretches, Q, STATE)
    query_c = out_c.reshape(stretches, Q, STATE)
    drive_c = driven.reshape(stretches, Q, heads, head_dim)
    scores = jnp.einsum("ctn,csn->cts", query_c, keys_b, preferred_element_type=jnp.float32)
    causal = jnp.asarray(np.tril(np.ones((Q, Q), bool)))[None, :, :, None]
    differ = cumul[:, :, None, :] - cumul[:, None, :, :]
    inner_wt = (
        jnp.where(causal, jnp.exp(jnp.where(causal, differ, 0.0)), 0.0)
        * scores[..., None]
        * level_wt[0]
    )
    inner_wt = inner_wt.astype(jnp.bfloat16)
    y_inner = jnp.einsum("ctsh,cshp->cthp", inner_wt, drive_c, preferred_element_type=jnp.float32)
    to_end = jnp.exp(totals[:, None, :] - cumul)
    weighted_b = (keys_b.astype(jnp.float32)[:, :, None, :] * to_end[..., None]).astype(
        jnp.bfloat16
    )
    states = jnp.einsum("cshn,cshp->chnp", weighted_b, drive_c, preferred_element_type=jnp.float32)
    local_bits = stretches.bit_length() - 1
    carried = jnp.zeros_like(states)
    block_states = states
    block_decay = totals
    stretch_ids = np.arange(stretches)
    for level in range(local_bits):
        span = 2**level
        repeated = jnp.repeat(block_states, span, axis=0)
        previous = jnp.concatenate(
            [jnp.zeros_like(repeated[:span]), repeated[: stretches - span]], 0
        )
        bit_set = jnp.asarray((stretch_ids >> level & 1).astype(np.float32))
        aligned = stretch_ids >> level << level
        factor = bit_set[:, None] * level_wt[level + 1] * jnp.exp(before - before[aligned])
        carried = carried + factor[:, :, None, None] * previous
        block_states = (
            block_states[0::2] * jnp.exp(block_decay[1::2])[:, :, None, None] + block_states[1::2]
        )
        block_decay = block_decay[0::2] + block_decay[1::2]
    block_state = block_states[0]
    block_total = block_decay[0]
    position = lax.axis_index("seq")
    cross_state = jnp.zeros_like(block_state)
    passed = jnp.zeros_like(block_total)
    seq_bits = lax.axis_size("seq").bit_length() - 1
    for level in range(seq_bits):
        other_state, other_total = (
            swapped(block_state.astype(jnp.bfloat16), "seq", level).astype(block_state.dtype),
            swapped(block_total.astype(jnp.bfloat16), "seq", level).astype(block_total.dtype),
        )
        upper = (jnp.right_shift(position, level) & 1).astype(jnp.float32)
        cross_state = (
            cross_state
            + upper
            * level_wt[local_bits + level + 1]
            * jnp.exp(passed)[:, None, None]
            * other_state
        )
        passed = passed + upper * other_total
        block_state = jnp.where(
            upper > 0.5,
            other_state * jnp.exp(block_total)[:, None, None] + block_state,
            block_state * jnp.exp(other_total)[:, None, None] + other_state,
        )
        block_total = block_total + other_total
    carried = carried + jnp.exp(before)[:, :, None, None] * cross_state[None]
    carried_low = carried.astype(jnp.bfloat16)
    y_cross = jnp.exp(cumul)[..., None] * jnp.einsum(
        "ctn,chnp->cthp", query_c, carried_low, preferred_element_type=jnp.float32
    )
    output = (
        y_inner
        + y_cross
        + d_skip[None, None, :, None]
        * values.astype(jnp.float32).reshape(stretches, Q, heads, head_dim)
    )
    output = output * lax.rsqrt(jnp.mean(output * output, axis=-1, keepdims=True) + 1e-05)
    places = (position * count + jnp.arange(count, dtype=jnp.int32)).reshape(stretches, Q)
    output = jnp.where((places < lengths[0])[:, :, None, None], output, 0.0)
    return output.reshape(1, count, inner).astype(jnp.bfloat16)


def solution(mesh):
    in_specs = (P("dp", "seq", None), P(("seq", "dp"), None), P(), P(), P(), P("dp", None), P("dp"))
    out_specs = P("dp", "seq", None)
    return jax.shard_map(body, mesh=mesh, in_specs=in_specs, out_specs=out_specs, check_vma=False)
```

profile of v0, /device:TPU:5, one launch (start us, length us, event | category | flops | bytes accessed | tf_op | source)
XLA Modules:
  0.0 375.2 jit_solution(5178389369494430748)
XLA Ops:
  9.6 133.8 %all-gather.2.cloned.1.call-done = bf16[4096,2336]{1,0:T(8,128)(2,1)} async-done(((bf16[16,2336]{1,0:T(8,128)(2,1)}), bf16[4096,2336]{1,0:T(8,128)(2,1)}) %all-gather.2.cloned.1.call-update) | async-done | bytes 19136528 | tf_op jit(solution)/shard_map/all_gather | solution.py:28
  143.4 18.0 %fusion.50 = (bf16[512,2336]{0,1:T(8,128)(2,1)S(1)}, f32[512,2336]{0,1:T(8,128)}) fusion(bf16[4096,2336]{1,0:T(8,128)(2,1)} %all-gather.2.cloned.1.call-done, bf16[1,512,4096]{2,1,0:T(8,128)(2,1)} %param.17), kind=kOutput, calls=%fused_computation.119 | convolution fusion | flops 9799090176 | bytes 30507008 | tf_op jit(solution)/shard_map/dot_general | solution.py:26
  162.6 6.3 %fusion.51 = f32[8,64,32]{2,0,1:T(8,128)S(1)} fusion(f32[8,64,32]{2,0,1:T(8,128)S(1)} %copy.43), kind=kOutput, calls=%fused_computation.120 | output fusion | flops 1032192 | bytes 131072 | tf_op jit(solution)/shard_map/jit(cumsum)/reduce_window_sum | solution.py:51
  170.4 3.1 collective-permute-start
  174.1 1.8 slice.189
  177.2 5.9 %fusion.44 = (bf16[512,2304]{0,1:T(8,128)(2,1)S(1)}, f32[512,2304]{0,1:T(8,128)}) fusion(f32[2304]{0:T(1024)S(1)} %get-tuple-element.7, bf16[512,2304]{0,1:T(8,128)(2,1)S(1)} %slice.189, f32[2304]{0:T(1024)S(1)} %get-tuple-element.8, bf16[3,2304]{0,1:T(8,128)(2,1)S(1)} %copy.40, f32[2304]{0:T(1024)S(1)} %get-tuple-element.6, f32[2304]{0:T(1024)S(1)} %get-tuple-element.5), kind=kLoop, calls=%fused_computation.113 | loop fusion | flops 24772608 | bytes 9487872 | tf_op jit(solution)/shard_map/convert.2
  183.9 5.3 %fusion.15 = f32[512,2048]{0,1:T(8,128)} fusion(f32[512,2304]{0,1:T(8,128)} %get-tuple-element.20), kind=kLoop, calls=%fused_computation.33 | loop fusion | flops 6291456 | bytes 8388608 | tf_op jit(solution)/shard_map/reshape | solution.py:48
  189.2 7.2 %reshape.221 = f32[8,64,32,64]{1,0,3,2:T(8,128)} reshape(f32[512,2048]{0,1:T(8,128)} %fusion.15) | data formatting | bytes 8388608 | tf_op jit(solution)/shard_map/reshape | solution.py:48
  196.4 6.3 %fusion.2 = f32[8,32,128,64]{2,3,1,0:T(8,128)S(1)} fusion(f32[8,64,32]{1,2,0:T(8,128)S(1)} %copy.49, f32[8,64,128]{2,1,0:T(8,128)S(1)} %convert_element_type.135, f32[8,64,32,64]{1,0,3,2:T(8,128)} %reshape.221, f32[8,64,32]{1,2,0:T(8,128)S(1)} %copy-done.11), kind=kOutput, calls=%fused_computation.13 | convolution fusion | flops 274726912 | bytes 12976128 | tf_op jit(solution)/shard_map/cshn,cshp->chnp/dot_general | solution.py:72
  203.2 2.8 copy-done
  206.2 1.4 fusion.30
  210.3 10.8 %collective-permute-done.2 = bf16[32]{0:T(256)(128)(2,1)S(1)} collective-permute-done((bf16[32]{0:T(256)(128)(2,1)S(1)}, bf16[32]{0:T(256)(128)(2,1)S(1)}, u32[]{:S(2)}, u32[]{:S(2)}) %collective-permute-start.2) | collective-permute-done | bytes 96 | tf_op jit(solution)/shard_map/ppermute | solution.py:20
  222.4 2.8 collective-permute-done.4
  227.2 2.3 fusion.42
  232.0 9.9 %collective-permute-done.3 = bf16[32,128,64]{1,2,0:T(8,128)(2,1)S(1)} collective-permute-done((bf16[32,128,64]{1,2,0:T(8,128)(2,1)}, bf16[32,128,64]{1,2,0:T(8,128)(2,1)S(1)}, u32[]{:S(2)}, u32[]{:S(2)}) %collective-permute-start.3) | collective-permute-done | bytes 524320 | tf_op jit(solution)/shard_map/ppermute | solution.py:20
  245.7 6.5 %collective-permute-done.6 = bf16[32]{0:T(256)(128)(2,1)S(1)} collective-permute-done((bf16[32]{0:T(256)(128)(2,1)S(1)}, bf16[32]{0:T(256)(128)(2,1)S(1)}, u32[]{:S(2)}, u32[]{:S(2)}) %collective-permute-start.6) | collective-permute-done | bytes 96 | tf_op jit(solution)/shard_map/ppermute | solution.py:20
  254.7 1.5 collective-permute-done.8
  257.3 2.1 fusion.37
  262.6 1.9 broadcast_multiply_fusion
  264.6 20.6 %collective-permute-done.7 = bf16[32,128,64]{1,2,0:T(8,128)(2,1)S(1)} collective-permute-done((bf16[32,128,64]{1,2,0:T(8,128)(2,1)}, bf16[32,128,64]{1,2,0:T(8,128)(2,1)S(1)}, u32[]{:S(2)}, u32[]{:S(2)}) %collective-permute-start.7) | collective-permute-done | bytes 524320 | tf_op jit(solution)/shard_map/ppermute | solution.py:20
  285.2 2.6 fusion.28
  287.8 3.0 collective-permute-start.9
  296.1 21.0 %collective-permute-done.9 = bf16[32,128,64]{1,2,0:T(8,128)(2,1)} collective-permute-done((bf16[32,128,64]{1,2,0:T(8,128)(2,1)}, bf16[32,128,64]{1,2,0:T(8,128)(2,1)}, u32[]{:S(2)}, u32[]{:S(2)}) %collective-permute-start.9) | collective-permute-done | bytes 524320 | tf_op jit(solution)/shard_map/ppermute | solution.py:20
  317.1 3.2 fusion.19
  320.3 4.0 %broadcast_in_dim.37 = f32[3,2,32,128,64]{3,4,2,1,0:T(8,128)} broadcast(f32[3,32,128,64]{2,3,1,0:T(8,128)S(1)} %slice-done.3), dimensions={0,2,3,4} | broadcast | bytes 9437184 | tf_op jit(solution)/shard_map/broadcast_in_dim | solution.py:80
  324.3 2.7 slice.172
  327.5 7.6 %add_convert_fusion = bf16[8,32,128,64]{2,3,1,0:T(8,128)(2,1)} fusion(f32[4,32,128,64]{2,3,1,0:T(8,128)} %slice.172, f32[6,32,128,64]{2,3,1,0:T(8,128)} %bitcast.73, f32[7,32,128,64]{2,3,1,0:T(8,128)S(1)} %slice-done, f32[32,128,64]{1,2,0:T(8,128)S(1)} %copy-done.4, f32[8,32]{1,0:T(8,128)S(1)} %get-tuple-element.9, f32[8,32]{1,0:T(8,128)S(1)} %get-tuple-element.30, ...), kind=kLoop, calls=%fused_computation.7 | loop fusion | flops 16777216 | bytes 23072768 | tf_op jit(solution)/shard_map/convert_element_type | solution.py:119
  335.1 3.5 fusion.53
  338.7 8.8 %multiply_reduce_fusion = (f32[8,64,32]{1,2,0:T(8,128)S(1)}, f32[8,64,32,64]{1,3,2,0:T(8,128)}) fusion(f32[8,64,32,64]{1,0,3,2:T(8,128)S(1)} %bitcast.70, f32[32]{0:T(128)S(1)} %copy-done.22, f32[8,64,32,64]{1,3,2,0:T(8,128)S(1)} %bitcast.72, f32[8,64,32]{1,2,0:T(8,128)S(1)} %copy-done.16, f32[]{:T(128)} %bitcast.4, f32[8,64,64]{2,1,0:T(8,128)S(1)} %copy-done.14, ...), kind=kOutput, calls=%fused_computation.6 | convolution fusion | flops 148881408 | bytes 12980356 | tf_op jit(solution)/shard_map/ctsh,cshp->cthp/dot_general | solution.py:67
  347.5 7.0 %select_convert_fusion = bf16[8,64,32,64]{1,3,2,0:T(8,128)(2,1)} fusion(f32[8,64,32,64]{1,3,2,0:T(8,128)} %get-tuple-element.60, f32[8,64,32]{1,2,0:T(8,128)S(1)} %add_rsqrt_fusion, pred[8,64]{1,0:T(8,128)(4,1)S(1)} %copy-done.17), kind=kLoop, calls=%fused_computation.5 | loop fusion | flops 3145728 | bytes 6357504 | tf_op jit(solution)/shard_map/convert_element_type | solution.py:132
  354.5 7.1 %copy.51 = bf16[8,64,32,64]{3,2,1,0:T(8,128)(2,1)} copy(bf16[8,64,32,64]{1,3,2,0:T(8,128)(2,1)} %select_convert_fusion) | data formatting | bytes 4194304 | tf_op jit(solution)/shard_map/convert_element_type | solution.py:132
  361.6 6.7 %convert_element_type.162 = bf16[1,512,2048]{2,1,0:T(8,128)(2,1)} reshape(bf16[8,64,32,64]{3,2,1,0:T(8,128)(2,1)} %copy.51) | data formatting | bytes 4194304 | tf_op jit(solution)/shard_map/convert_element_type | solution.py:132
  (120 shorter events, 30.4 us)
Async XLA Ops:
  6.5 136.9 %all-gather.2.cloned.1.call-start = ((), (), s32[]{:S(2)}) async-start(), calls=%async_computation | async-start | bytes 20000768 | tf_op jit(solution)/shard_map/all_gather | solution.py:28
  9.6 151.7 %copy-start.20 = (f32[32]{0:T(128)S(1)}, f32[32]{0:T(128)}, u32[]{:S(2)}) copy-start(f32[32]{0:T(128)} %param.20) | copy-start | bytes 388
  161.4 12.2 %copy-start.6 = (bf16[512,2336]{0,1:T(8,128)(2,1)}, bf16[512,2336]{0,1:T(8,128)(2,1)S(1)}, u32[]{:S(2)}) copy-start(bf16[512,2336]{0,1:T(8,128)(2,1)S(1)} %get-tuple-element.57) | copy-start | bytes 7176196
  169.9 36.3 %copy-start.19 = (f32[32]{0:T(128)}, f32[32]{0:T(128)S(1)}, u32[]{:S(2)}) copy-start(f32[32]{0:T(128)S(1)} %exponential_bitcast_fusion) | copy-start | bytes 388
  170.4 6.3 %copy-start.10 = (f32[8,64,32]{2,0,1:T(8,128)S(1)}, f32[8,64,32]{2,0,1:T(8,128)}, u32[]{:S(2)}) copy-start(f32[8,64,32]{2,0,1:T(8,128)} %get-tuple-element.28) | copy-start | bytes 196612
  170.4 6.4 %collective-permute-start = (bf16[3,2304]{1,0:T(4,128)(2,1)S(1)}, bf16[3,2304]{1,0:T(4,128)(2,1)S(1)}, u32[]{:S(2)}, u32[]{:S(2)}) collective-permute-start(bf16[3,2304]{1,0:T(4,128)(2,1)S(1)} %copy.39), channel_id=1, source_target_pairs={{0,8},{8,16},{16,24},{24,32},{32,40},{40,48},{48,56},{56,64},{64,7... | collective-permute-start | bytes 41480 | tf_op jit(solution)/shard_map/ppermute | solution.py:14
  174.1 47.1 %copy-start.18 = (f32[1,32]{1,0:T(1,128)}, f32[1,32]{1,0:T(1,128)S(1)}, u32[]{:S(2)}) copy-start(f32[1,32]{1,0:T(1,128)S(1)} %get-tuple-element.18) | copy-start | bytes 388
  189.2 7.2 %copy-start.11 = (f32[8,64,32]{1,2,0:T(8,128)S(1)}, f32[8,64,32]{1,2,0:T(8,128)}, u32[]{:S(2)}) copy-start(f32[8,64,32]{1,2,0:T(8,128)} %copy.41) | copy-start | bytes 196612
  208.2 18.2 %collective-permute-start.1 = (bf16[32,128,64]{1,2,0:T(8,128)(2,1)S(1)}, bf16[32,128,64]{1,2,0:T(8,128)(2,1)S(1)}, u32[]{:S(2)}, u32[]{:S(2)}) collective-permute-start(bf16[32,128,64]{1,2,0:T(8,128)(2,1)S(1)} %get-tuple-element.25), channel_id=1, source_target_pairs={{0,8},{8,0},{16,24},{24,16},{32,40},{40,32},{48,56},{56,48},{64,72... | collective-permute-start | bytes 1572872 | tf_op jit(solution)/shard_map/ppermute | solution.py:20
  208.6 12.6 %collective-permute-start.2 = (bf16[32]{0:T(256)(128)(2,1)S(1)}, bf16[32]{0:T(256)(128)(2,1)S(1)}, u32[]{:S(2)}, u32[]{:S(2)}) collective-permute-start(bf16[32]{0:T(256)(128)(2,1)S(1)} %bitcast_convert_fusion), channel_id=1, source_target_pairs={{0,8},{8,0},{16,24},{24,16},{32,40},{40,32},{48,56},{56,48},{64,72... | collective-permute-start | bytes 200 | tf_op jit(solution)/shard_map/ppermute | solution.py:20
  221.2 4.0 %collective-permute-start.4 = (bf16[32]{0:T(256)(128)(2,1)S(1)}, bf16[32]{0:T(256)(128)(2,1)}, u32[]{:S(2)}, u32[]{:S(2)}) collective-permute-start(bf16[32]{0:T(256)(128)(2,1)S(1)} %fusion.36), channel_id=1, source_target_pairs={{0,16},{8,24},{16,0},{24,8},{32,48},{40,56},{48,32},{56,40},{64,80... | collective-permute-start | bytes 200 | tf_op jit(solution)/shard_map/ppermute | solution.py:20
  229.5 63.7 %copy-start.9 = (f32[8,64,32]{2,0,1:T(8,128)S(1)}, f32[8,64,32]{2,0,1:T(8,128)}, u32[]{:S(2)}) copy-start(f32[8,64,32]{2,0,1:T(8,128)} %get-tuple-element.27) | copy-start | bytes 196612
  229.5 12.4 %collective-permute-start.3 = (bf16[32,128,64]{1,2,0:T(8,128)(2,1)}, bf16[32,128,64]{1,2,0:T(8,128)(2,1)S(1)}, u32[]{:S(2)}, u32[]{:S(2)}) collective-permute-start(bf16[32,128,64]{1,2,0:T(8,128)(2,1)} %get-tuple-element.15), channel_id=1, source_target_pairs={{0,16},{8,24},{16,0},{24,8},{32,48},{40,56},{48,32},{56,40},{64,80... | collective-permute-start | bytes 1572872 | tf_op jit(solution)/shard_map/ppermute | solution.py:20
  241.9 52.2 %copy-start.2 = (bf16[32,128,64]{1,2,0:T(8,128)(2,1)}, bf16[32,128,64]{1,2,0:T(8,128)(2,1)S(1)}, u32[]{:S(2)}) copy-start(bf16[32,128,64]{1,2,0:T(8,128)(2,1)S(1)} %collective-permute-done.3) | copy-start | bytes 1572868
  242.3 15.1 %collective-permute-start.5 = (bf16[32,128,64]{1,2,0:T(8,128)(2,1)S(1)}, bf16[32,128,64]{1,2,0:T(8,128)(2,1)S(1)}, u32[]{:S(2)}, u32[]{:S(2)}) collective-permute-start(bf16[32,128,64]{1,2,0:T(8,128)(2,1)S(1)} %fusion.38), channel_id=1, source_target_pairs={{0,32},{8,40},{16,48},{24,56},{32,0},{40,8},{48,16},{56,24},{64,96... | collective-permute-start | bytes 1572872 | tf_op jit(solution)/shard_map/ppermute | solution.py:20
  244.0 8.2 %collective-permute-start.6 = (bf16[32]{0:T(256)(128)(2,1)S(1)}, bf16[32]{0:T(256)(128)(2,1)S(1)}, u32[]{:S(2)}, u32[]{:S(2)}) collective-permute-start(bf16[32]{0:T(256)(128)(2,1)S(1)} %convert_element_type.151), channel_id=1, source_target_pairs={{0,32},{8,40},{16,48},{24,56},{32,0},{40,8},{48,16},{56,24},{64,96... | collective-permute-start | bytes 200 | tf_op jit(solution)/shard_map/ppermute | solution.py:20
  252.8 3.3 collective-permute-start.8
  257.3 36.8 %copy-start.3 = (bf16[32,128,64]{1,2,0:T(8,128)(2,1)}, bf16[32,128,64]{1,2,0:T(8,128)(2,1)S(1)}, u32[]{:S(2)}) copy-start(bf16[32,128,64]{1,2,0:T(8,128)(2,1)S(1)} %collective-permute-done.5) | copy-start | bytes 1572868
  259.4 25.7 %collective-permute-start.7 = (bf16[32,128,64]{1,2,0:T(8,128)(2,1)}, bf16[32,128,64]{1,2,0:T(8,128)(2,1)S(1)}, u32[]{:S(2)}, u32[]{:S(2)}) collective-permute-start(bf16[32,128,64]{1,2,0:T(8,128)(2,1)} %fusion.37), channel_id=1, source_target_pairs={{0,64},{8,72},{16,80},{24,88},{32,96},{40,104},{48,112},{56,120},{... | collective-permute-start | bytes 1572872 | tf_op jit(solution)/shard_map/ppermute | solution.py:20
  287.8 29.3 %collective-permute-start.9 = (bf16[32,128,64]{1,2,0:T(8,128)(2,1)}, bf16[32,128,64]{1,2,0:T(8,128)(2,1)}, u32[]{:S(2)}, u32[]{:S(2)}) collective-permute-start(bf16[32,128,64]{1,2,0:T(8,128)(2,1)} %fusion.28), channel_id=1, source_target_pairs={{0,128},{8,136},{16,144},{24,152},{32,160},{40,168},{48,176},{56,1... | collective-permute-start | bytes 1572872 | tf_op jit(solution)/shard_map/ppermute | solution.py:20
  294.1 26.1 %slice-start.3 = ((f32[4,32,128,64]{2,3,1,0:T(8,128)}), f32[3,32,128,64]{2,3,1,0:T(8,128)S(1)}, s32[]{:S(2)}) async-start(f32[4,32,128,64]{2,3,1,0:T(8,128)} %copy-done.1), calls=%async_computation.4 | async-start | bytes 6291456 | tf_op jit(solution)/shard_map/slice | solution.py:82
  320.3 4.0 %copy-start.5 = (f32[32,128,64]{1,2,0:T(8,128)S(1)}, f32[32,128,64]{1,2,0:T(8,128)}, u32[]{:S(2)}) copy-start(f32[32,128,64]{1,2,0:T(8,128)} %get-tuple-element.26) | copy-start | bytes 3145732
  320.3 6.7 %slice-start = ((f32[8,32,128,64]{2,3,1,0:T(8,128)}), f32[7,32,128,64]{2,3,1,0:T(8,128)S(1)}, s32[]{:S(2)}) async-start(f32[8,32,128,64]{2,3,1,0:T(8,128)} %copy-done), calls=%async_computation.1 | async-start | bytes 14680064 | tf_op jit(solution)/shard_map/slice | solution.py:82
  324.3 14.3 %slice-start.1 = ((s8[8388608]{0:T(1024)(128)(4,1)}), s8[4194304]{0:T(1024)(128)(4,1)S(1)}, s32[]{:S(2)}) async-start(s8[8388608]{0:T(1024)(128)(4,1)} %bitcast.69), calls=%async_computation.2 | async-start | bytes 8388608
  327.5 11.2 %slice-start.2 = ((s8[8388608]{0:T(1024)(128)(4,1)}), s8[4194304]{0:T(1024)(128)(4,1)S(1)}, s32[]{:S(2)}) async-start(s8[8388608]{0:T(1024)(128)(4,1)} %bitcast.69), calls=%async_computation.3 | async-start | bytes 8388608
  335.1 3.5 copy-start.12
  335.1 3.6 copy-start.14
  335.1 3.6 copy-start.15
  335.1 3.6 copy-start.16
  335.1 3.6 copy-start.22
  335.1 3.6 copy-start.23
  338.7 8.8 %copy-start.17 = (pred[8,64]{1,0:T(8,128)(4,1)S(1)}, pred[8,64]{1,0:T(8,128)(4,1)}, u32[]{:S(2)}) copy-start(pred[8,64]{1,0:T(8,128)(4,1)} %add_compare_fusion) | copy-start | bytes 1540
  (7 other events, 14.3 us)
Sparse Core Ops, SparseCore 0:
  10.9 132.4 all-gather.1
where the time goes:
time: 376 us; the launch traced here: 375 us
  waiting for transfers between devices  208 us (55%)
  other arithmetic  56.9 us (15%)
  local copies, waits for them, and re-layouts  43.1 us (11%)
  matrix products  37.4 us (10%)
  between operations  17.3 us (5%)
  starting transfers between devices  12.8 us (3%)
    all_gather x1, waiting for transfers between devices, body(): lax.all_gather(w_in, ('seq', 'dp'), axis=0, tiled=True)  134 us
    ppermute x9, waiting for transfers between devices, swapped(): return lax.ppermute(value, axis, pairs)  73.2 us
    dot_general x1, matrix products, body(): jnp.dot(token_rows, lax.all_gather(w_in, ('seq', 'dp'), axis=0, tiled=Tru...  18 us
    convert_element_type x2, local copies, waits for them, and re-layouts, body(): return output.reshape(1, count, inner).astype(jnp.bfloat16)  13.9 us
    ppermute x9, starting transfers between devices, swapped(): return lax.ppermute(value, axis, pairs)  9.71 us
    dot_general x1, matrix products, body(): jnp.einsum('ctsh,cshp->cthp', inner_wt, drive_c, preferred_element_type=j...  8.75 us
    convert_element_type x5, other arithmetic, body(): block_state.astype(jnp.bfloat16)  8.74 us
    convert_element_type x1, other arithmetic, body(): carried_low = carried.astype(jnp.bfloat16)  7.62 us
  transfers between devices with their start and end apart: 11, of which 8 were waited for; matrix products, arithmetic and copies ran while one was open for 5% of the time, Pallas kernels for 0%

commit v1 on v0

v1 whole, which is shorter than its diff:
```python
import jax
import jax.numpy as jnp
from jax import lax
from jax.experimental import pallas as pl
from jax.experimental.pallas import tpu as pltpu
from jax.sharding import PartitionSpec as P

STATE = 128
Q = 64
HALO = 16
WIDE = 256
ROWS = 80
F32 = jnp.float32
BF16 = jnp.bfloat16


def dot(a, b):
    return jnp.dot(a, b, preferred_element_type=F32)


def two_parts(x):
    high = x.astype(BF16)
    return high, (x - high.astype(F32)).astype(BF16)


def spread(block, width):
    head = lax.broadcasted_iota(jnp.int32, (2 * 128, width), 0) & 127
    lane = lax.broadcasted_iota(jnp.int32, (2 * 128, width), 1)
    return jnp.where(head == 4 * block + (lane >> 6), 1.0, 0.0).astype(BF16)


def mix_kernel(
    level_ref, tok_ref, w_ref, conv_ref, rate_ref, skip_ref,
    part_ref, send_ref, query_ref, grow_ref,
    proj_s, raw_s, score_s, keys_s, step_s, fade_s, sums_s, sums_t, total_s,
):
    count = part_ref.shape[0]
    step = pl.program_id(0)
    block = step - 2
    proj_s[...] = dot(tok_ref[...], w_ref[...])

    def convolve():
        raw_s[...] = proj_s[...].astype(BF16).astype(F32)
        taps = conv_ref.shape[0]
        total = None
        for tap in range(taps):
            part = raw_s[pl.ds(HALO - taps + 1 + tap, count), :] * conv_ref[tap : tap + 1, :]
            total = part if total is None else total + part
        return total

    @pl.when(step == 0)
    def _():
        mixed = convolve().astype(BF16)
        keys = mixed[:, :STATE]
        query = mixed[:, STATE:]
        query_ref[...] = query
        keys_t = keys.astype(F32).T.astype(BF16)
        keys_s[...] = keys_t
        row = lax.broadcasted_iota(jnp.int32, (count, count), 0)
        col = lax.broadcasted_iota(jnp.int32, (count, count), 1)
        apart = (row >> 6) ^ (col >> 6)
        weight = jnp.where(
            apart == 0,
            level_ref[0],
            jnp.where(apart == 1, level_ref[1], jnp.where(apart < 4, level_ref[2], level_ref[3])),
        )
        score_s[...] = dot(query, keys_t) * jnp.where(col <= row, weight, 0.0)

    @pl.when(step == 1)
    def _():
        x = proj_s[pl.ds(HALO, count), :128]
        lane = lax.broadcasted_iota(jnp.int32, x.shape, 1)
        x = jnp.where(lane < 32, x, 0.0)
        size = jnp.maximum(x, 0.0) + jnp.log1p(jnp.exp(-jnp.abs(x)))
        decay = -size * rate_ref[...]
        row = lax.broadcasted_iota(jnp.int32, (count, count), 0)
        col = lax.broadcasted_iota(jnp.int32, (count, count), 1)
        lower = jnp.where(col <= row, 1.0, 0.0).astype(BF16)
        first = decay.astype(BF16)
        rest = decay - first.astype(F32)
        second = rest.astype(BF16)
        third = (rest - second.astype(F32)).astype(BF16)
        sums = dot(lower, first) + dot(lower, second) + dot(lower, third)
        turned = sums.T
        for group in range(8):
            sums_t[group] = turned[4 * group : 4 * group + 8]
            sums_s[group] = sums if group == 0 else pltpu.roll(sums, 128 - 4 * group, 1)
        high, low = two_parts(size)
        step_s[:, :128] = high
        step_s[:, 128:] = low
        high, low = two_parts(jnp.exp(sums[count - 1 :] - sums))
        fade_s[:, :128] = high
        fade_s[:, 128:] = low
        high, low = two_parts(jnp.exp(sums))
        grow_ref[:, :128] = high
        grow_ref[:, 128:] = low
        total = jnp.broadcast_to(sums[count - 1 :], (16, 128))
        first = total.astype(BF16)
        rest = total - first.astype(F32)
        second = rest.astype(BF16)
        third = (rest - second.astype(F32)).astype(BF16)
        place = lax.broadcasted_iota(jnp.int32, total.shape, 0)
        total_s[...] = jnp.where(
            place == 0,
            first.astype(F32),
            jnp.where(place == 1, second.astype(F32), jnp.where(place == 2, third.astype(F32), 0.0)),
        ).astype(BF16)

    @pl.when(step >= 2)
    def _():
        convolved = convolve()
        values = (convolved * jax.nn.sigmoid(convolved)).astype(BF16).astype(F32)
        lanes = spread(block, WIDE)
        driven = (values * dot(step_s[...], lanes)).astype(BF16)
        faded = (driven.astype(F32) * dot(fade_s[...], lanes)).astype(BF16)
        states = dot(keys_s[...], faded).astype(BF16)
        totals = dot(total_s[...], lanes[:128]).astype(BF16)
        for unit in range(4):
            pair, half = unit // 2, unit % 2
            send_ref[unit, :64] = states[half * 64 : half * 64 + 64, pair * 128 : pair * 128 + 128]
            send_ref[unit, 64:] = totals[:, pair * 128 : pair * 128 + 128]
        side = lax.broadcasted_iota(jnp.int32, (count, 128), 1) < 64
        skipped = values * skip_ref[...]
        for pair in range(2):
            both = driven[:, pair * 128 : pair * 128 + 128]
            sides = (
                jnp.where(side, both, jnp.zeros_like(both)),
                jnp.where(side, jnp.zeros_like(both), both),
            )
            for tile in range(count // 128):
                top, reach = tile * 128, tile * 128 + 128
                total = skipped[top:reach, pair * 128 : pair * 128 + 128]
                score = score_s[top:reach, :reach]
                for half in range(2):
                    head = 2 * pair + half
                    later = sums_s[block, top:reach, head : head + 1]
                    earlier = sums_t[block, head : head + 1, :reach]
                    weight = score * jnp.exp(jnp.minimum(later - earlier, 0.0))
                    total = total + dot(weight.astype(BF16), sides[half][:reach])
                part_ref[top:reach, pair * 128 : pair * 128 + 128] = total


def scan_kernel(level_ref, state_ref, out_ref, sum_s, block_s):
    count = state_ref.shape[0]
    totals = []
    for place in range(count):
        rows = state_ref[place, 64:80].astype(F32)
        totals.append(rows[0:1] + rows[1:2] + rows[2:3])
    before = [jnp.zeros_like(totals[0])]
    for place in range(count - 1):
        before.append(before[-1] + totals[place])
    sum_s[...] = jnp.zeros_like(sum_s)
    for place in range(count):
        block_s[place] = state_ref[place, :64].astype(F32)
    level = 0
    while (1 << level) < count:
        span = 1 << level
        for start in range(span, count, 2 * span):
            previous = block_s[start - span] * level_ref[4 + level]
            for place in range(start, start + span):
                sum_s[place] += jnp.exp(before[place] - before[start]) * previous
            end = start + span
            gone = totals[start]
            for place in range(start + 1, end):
                gone = gone + totals[place]
            block_s[start - span] = block_s[start - span] * jnp.exp(gone) + block_s[start]
        level += 1
    out_ref[...] = sum_s[...].astype(BF16)


def finish_kernel(place_ref, part_ref, state_ref, query_ref, grow_ref, out_ref):
    count = part_ref.shape[0]
    block = pl.program_id(0)
    grow = dot(grow_ref[...], spread(block, WIDE))
    first = lax.broadcasted_iota(jnp.int32, (2 * 128, 128), 0) & 127
    second = lax.broadcasted_iota(jnp.int32, (2 * 128, 128), 1)
    ones = jnp.where((first >> 6) == (second >> 6), 1.0, 0.0).astype(BF16)
    live = place_ref[0] + lax.broadcasted_iota(jnp.int32, (count, 128), 0) < place_ref[1]
    for pair in range(2):
        lanes = slice(pair * 128, pair * 128 + 128)
        state = jnp.concatenate([state_ref[2 * pair], state_ref[2 * pair + 1]], 0)
        y = part_ref[:, lanes] + grow[:, lanes] * dot(query_ref[...], state)
        high, low = two_parts(y * y)
        mean = dot(jnp.concatenate([high, low], 1), ones) * (1.0 / 64.0)
        y = y * lax.rsqrt(mean + 1e-05)
        out_ref[:, lanes] = jnp.where(live, y, 0.0).astype(BF16)


def params():
    return pltpu.CompilerParams(dimension_semantics=("arbitrary",), vmem_limit_bytes=56 * 2**20)


def body(tokens, w_in, conv_w, a_rate, d_skip, level_w, lengths):
    token_rows = tokens.reshape(-1, tokens.shape[-1])
    count, width = token_rows.shape
    taps, channels = conv_w.shape
    heads = a_rate.shape[0]
    inner = channels - 2 * STATE
    head_dim = inner // heads
    blocks = inner // WIDE
    ring = lax.axis_size("seq")
    position = lax.axis_index("seq")
    rim = lax.ppermute(token_rows[count - HALO :], "seq", [(i, i + 1) for i in range(ring - 1)])
    padded = jnp.concatenate([rim, token_rows], 0)
    levels = jnp.concatenate(
        [level_w.reshape(-1).astype(F32) / 256.0, jnp.zeros((16 - level_w.shape[-1],), F32)]
    )
    rate = jnp.concatenate([a_rate, jnp.zeros((128 - heads,), F32)])[None]
    skip = jnp.repeat(d_skip, head_dim)[None]
    weights = lax.all_gather(w_in, ("seq", "dp"), axis=0, tiled=True)
    smem = pl.BlockSpec(memory_space=pltpu.SMEM)

    def column(i):
        return jnp.where(i < 2, blocks + i, i - 2)

    def head_block(i):
        return jnp.maximum(i - 2, 0)

    part, send, query, grow = pl.pallas_call(
        mix_kernel,
        out_shape=(
            jax.ShapeDtypeStruct((count, inner), F32),
            jax.ShapeDtypeStruct((heads, ROWS, 128), BF16),
            jax.ShapeDtypeStruct((count, STATE), BF16),
            jax.ShapeDtypeStruct((count, 256), BF16),
        ),
        grid=(blocks + 2,),
        in_specs=[
            smem,
            pl.BlockSpec((count + HALO, width), lambda i: (0, 0), pipeline_mode=pl.Buffered(1)),
            pl.BlockSpec((width, WIDE), lambda i: (0, column(i))),
            pl.BlockSpec((taps, WIDE), lambda i: (0, jnp.minimum(column(i), blocks))),
            pl.BlockSpec((1, 128), lambda i: (0, 0)),
            pl.BlockSpec((1, WIDE), lambda i: (0, head_block(i))),
        ],
        out_specs=(
            pl.BlockSpec((count, WIDE), lambda i: (0, head_block(i))),
            pl.BlockSpec((4, ROWS, 128), lambda i: (head_block(i), 0, 0)),
            pl.BlockSpec((count, STATE), lambda i: (0, 0)),
            pl.BlockSpec((count, 256), lambda i: (0, 0)),
        ),
        scratch_shapes=[
            pltpu.VMEM((count + HALO, WIDE), F32),
            pltpu.VMEM((count + HALO, WIDE), F32),
            pltpu.VMEM((count, count), F32),
            pltpu.VMEM((STATE, count), BF16),
            pltpu.VMEM((count, 256), BF16),
            pltpu.VMEM((count, 256), BF16),
            pltpu.VMEM((8, count, 128), F32),
            pltpu.VMEM((8, 8, count), F32),
            pltpu.VMEM((16, 128), BF16),
        ],
        compiler_params=params(),
        name="mix",
    )(levels, padded, weights, conv_w, rate, skip)

    gathered = lax.all_to_all(send, "seq", 0, 0, tiled=True)
    scanned = pl.pallas_call(
        scan_kernel,
        out_shape=jax.ShapeDtypeStruct((ring, 64, 128), BF16),
        in_specs=[smem, pl.BlockSpec(memory_space=pltpu.VMEM)],
        out_specs=pl.BlockSpec(memory_space=pltpu.VMEM),
        scratch_shapes=[pltpu.VMEM((ring, 64, 128), F32), pltpu.VMEM((ring, 64, 128), F32)],
        compiler_params=pltpu.CompilerParams(vmem_limit_bytes=32 * 2**20),
        name="scan",
    )(levels, gathered)
    carried = lax.all_to_all(scanned, "seq", 0, 0, tiled=True)

    places = jnp.stack([position * count, lengths[0]]).astype(jnp.int32)
    output = pl.pallas_call(
        finish_kernel,
        out_shape=jax.ShapeDtypeStruct((count, inner), BF16),
        grid=(blocks,),
        in_specs=[
            smem,
            pl.BlockSpec((count, WIDE), lambda i: (0, i)),
            pl.BlockSpec((4, 64, 128), lambda i: (i, 0, 0)),
            pl.BlockSpec((count, STATE), lambda i: (0, 0)),
            pl.BlockSpec((count, 256), lambda i: (0, 0)),
        ],
        out_specs=pl.BlockSpec((count, WIDE), lambda i: (0, i)),
        compiler_params=params(),
        name="finish",
    )(places, part, carried, query, grow)
    return output.reshape(1, count, inner)


def solution(mesh):
    in_specs = (P("dp", "seq", None), P(("seq", "dp"), None), P(), P(), P(), P("dp", None), P("dp"))
    out_specs = P("dp", "seq", None)
    return jax.shard_map(body, mesh=mesh, in_specs=in_specs, out_specs=out_specs, check_vma=False)
```

time: 376 us -> 243 us (0.65)
  waiting for transfers between devices: 208 us -> 139 us
  other arithmetic: 56.9 us -> 6.03 us
  Pallas kernels: 0 us -> 42.7 us
  local copies, waits for them, and re-layouts: 43.1 us -> 4.95 us
  matrix products: 37.4 us -> 0 us
  blocking collectives: 0 us -> 26 us
  starting transfers between devices: 12.8 us -> 8.41 us
    ppermute x10 -> x1, waiting for transfers between devices: 73.2 us -> 0.01 us  [body(): lax.ppermute(token_rows[count - HALO:], 'seq', [(i, i + 1) for i in range...]
    pallas_call x0 -> x3, Pallas kernels: none -> 42.7 us  [the longest x1 32.2 us: body(): pl.pallas_call(mix_kernel, out_shape=(jax.ShapeDtypeStruct((count, inner)...]
    dot_general x4 -> x0, matrix products: 33.9 us -> none  [the longest x1 18 us: body(): jnp.dot(token_rows, lax.all_gather(w_in, ('seq', 'dp'), axis=0, tiled=Tru...]
    all_to_all x0 -> x1, blocking collectives: none -> 26 us  [body(): gathered = lax.all_to_all(send, 'seq', 0, 0, tiled=True)]
    convert_element_type x11 -> x0, other arithmetic: 24 us -> none  [the longest x5 8.74 us: body(): block_state.astype(jnp.bfloat16)]
    all_to_all x0 -> x1, waiting for transfers between devices: none -> 14.3 us  [body(): carried = lax.all_to_all(scanned, 'seq', 0, 0, tiled=True)]
    convert_element_type x2 -> x0, local copies, waits for them, and re-layouts: 13.9 us -> none  [body(): return output.reshape(1, count, inner).astype(jnp.bfloat16)]
    another operation x3 -> x1, other arithmetic: 12.3 us -> 0.64 us  [body(): places = jnp.stack([position * count, lengths[0]]).astype(jnp.int32)]
  transfers between devices with their start and end apart: 11 -> 3, of which waited for: 8 -> 2; matrix products, arithmetic and copies ran while one was open for 5% -> 4% of each run, Pallas kernels for 0% -> 0%
where the time goes in v1:
time: 243 us; the launch traced here: 241 us
  waiting for transfers between devices  139 us (57%)
  Pallas kernels  42.7 us (18%)
  blocking collectives  26 us (11%)
  between operations  14.1 us (6%)
  starting transfers between devices  8.41 us (3%)
  other arithmetic  6.03 us (2%)
  local copies, waits for them, and re-layouts  4.95 us (2%)
    all_gather x1, waiting for transfers between devices, body(): weights = lax.all_gather(w_in, ('seq', 'dp'), axis=0, tiled=True)  124 us
    pallas_call x1, Pallas kernels, body(): pl.pallas_call(mix_kernel, out_shape=(jax.ShapeDtypeStruct((count, inner)...  32.2 us
    all_to_all x1, blocking collectives, body(): gathered = lax.all_to_all(send, 'seq', 0, 0, tiled=True)  26 us
    all_to_all x1, waiting for transfers between devices, body(): carried = lax.all_to_all(scanned, 'seq', 0, 0, tiled=True)  14.3 us
    pallas_call x1, Pallas kernels, body(): pl.pallas_call(finish_kernel, out_shape=jax.ShapeDtypeStruct((count, inne...  8.74 us
    all_to_all x1, starting transfers between devices, body(): carried = lax.all_to_all(scanned, 'seq', 0, 0, tiled=True)  5.58 us
  transfers between devices with their start and end apart: 3, of which 2 were waited for; matrix products, arithmetic and copies ran while one was open for 4% of the time, Pallas kernels for 0%

profile of v1, /device:TPU:5, one launch (start us, length us, event | category | flops | bytes accessed | tf_op | source)
XLA Modules:
  0.0 240.8 jit_solution(9178558413684423041)
XLA Ops:
  6.5 0.0 all-gather.2.cloned.1.call-start
  6.5 0.7 all-gather.2.cloned.1.call-update
  7.3 0.9 slice_bitcast_fusion
  8.2 2.8 %collective-permute-start = (bf16[16,4096]{1,0:T(8,128)(2,1)S(1)}, bf16[16,4096]{1,0:T(8,128)(2,1)S(1)}, u32[]{:S(2)}, u32[]{:S(2)}) collective-permute-start(bf16[16,4096]{1,0:T(8,128)(2,1)S(1)} %slice_bitcast_fusion), channel_id=1, source_target_pairs={{0,8},{8,16},{16,24},{24,32},{32,40},{40,48},{48,56},{56,64},{64,7... | collective-permute-start | bytes 393224 | tf_op jit(solution)/shard_map/ppermute | solution.py:203
  11.0 0.7 multiply_bitcast_fusion
  11.7 0.7 broadcast_in_dim.8
  12.4 0.7 broadcast_in_dim_reshape.3.skip_ref
  13.1 0.6 concatenate.9.level_ref
  13.7 1.2 pad_bitcast_fusion.rate_ref
  14.9 0.0 collective-permute-done
  14.9 4.7 %pad_maximum_fusion.tok_ref = bf16[528,4096]{1,0:T(8,128)(2,1)} fusion(bf16[512,4096]{1,0:T(8,128)(2,1)} %bitcast.9, bf16[16,4096]{1,0:T(8,128)(2,1)S(1)} %collective-permute-done), kind=kLoop, calls=%fused_computation | loop fusion | flops 8650752 | bytes 8650752 | tf_op jit(solution)/shard_map/concatenate | solution.py:204
  19.6 0.0 copy-start
  19.6 123.8 %all-gather.2.cloned.1.call-done.w_ref = bf16[4096,2336]{1,0:T(8,128)(2,1)} async-done(((bf16[16,2336]{1,0:T(8,128)(2,1)}), bf16[4096,2336]{1,0:T(8,128)(2,1)}) %all-gather.2.cloned.1.call-update) | async-done | bytes 19136528 | tf_op jit(solution)/shard_map/all_gather | solution.py:210
  143.4 32.2 %mix.1 = (f32[512,2048]{1,0:T(8,128)}, bf16[32,80,128]{2,1,0:T(8,128)(2,1)}, bf16[512,128]{1,0:T(8,128)(2,1)}, bf16[512,256]{1,0:T(8,128)(2,1)}) custom-call(f32[16]{0:T(128)} %concatenate.9.level_ref, bf16[528,4096]{1,0:T(8,128)(2,1)} %pad_maximum_fusion.tok_ref, bf16[4096,2336]{1,0:T(8,128)(2,1)} %all-gather.2.cloned.1.call-done.w_ref, ...), custom_call_target="tpu_custom_call" | custom-call | tf_op jit(solution)/shard_map/mix/pallas_call | solution.py:219
  175.6 26.0 %all_to_all.10.state_ref = bf16[32,80,128]{2,1,0:T(8,128)(2,1)S(1)} all-to-all(bf16[32,80,128]{2,1,0:T(8,128)(2,1)} %get-tuple-element.10), channel_id=1, replica_groups=mesh['seq'=32,'dp'=8] {'seq'}, dimensions={0} | all-to-all | bytes 1310720 | tf_op jit(solution)/shard_map/all_to_all | solution.py:257
  201.6 0.0 copy-done
  201.6 1.7 scan.1
  203.3 5.6 %all-to-all-start.1 = ((bf16[32,64,128]{2,1,0:T(8,128)(2,1)}), bf16[32,64,128]{2,1,0:T(8,128)(2,1)S(1)}, u32[]{:S(2)}, u32[]{:S(2)}) async-start(bf16[32,64,128]{2,1,0:T(8,128)(2,1)} %scan.1), calls=%async_computation.1 | async-start | bytes 1048576 | tf_op jit(solution)/shard_map/all_to_all | solution.py:267
  209.5 0.6 pad_add_fusion.place_ref
  210.2 14.3 %all-to-all-done.1.state_ref = bf16[32,64,128]{2,1,0:T(8,128)(2,1)S(1)} async-done(((bf16[32,64,128]{2,1,0:T(8,128)(2,1)}), bf16[32,64,128]{2,1,0:T(8,128)(2,1)S(1)}, u32[]{:S(2)}, u32[]{:S(2)}) %all-to-all-start.1) | async-done | bytes 524320 | tf_op jit(solution)/shard_map/all_to_all | solution.py:267
  224.4 0.0 copy-start.1
  224.4 0.8 copy-done.1
  225.2 8.7 %finish.1 = bf16[512,2048]{1,0:T(8,128)(2,1)} custom-call(s32[2]{0:T(128)} %pad_add_fusion.place_ref, f32[512,2048]{1,0:T(8,128)} %get-tuple-element.9.part_ref, bf16[32,64,128]{2,1,0:T(8,128)(2,1)} %copy-done.1, bf16[512,128]{1,0:T(8,128)(2,1)} %get-tuple-element.11.query_ref, bf16[512,256]{1,0:T(8,128)(2,1)} %get-tuple-element.12.grow_ref), custom_call_target="tpu_custom_call" | custom-call | tf_op jit(solution)/shard_map/finish/pallas_call | solution.py:270
Async XLA Ops:
  6.5 136.9 %all-gather.2.cloned.1.call-start = ((), (), s32[]{:S(2)}) async-start(), calls=%async_computation.2 | async-start | bytes 20000768 | tf_op jit(solution)/shard_map/all_gather | solution.py:210
  8.2 6.7 %collective-permute-start = (bf16[16,4096]{1,0:T(8,128)(2,1)S(1)}, bf16[16,4096]{1,0:T(8,128)(2,1)S(1)}, u32[]{:S(2)}, u32[]{:S(2)}) collective-permute-start(bf16[16,4096]{1,0:T(8,128)(2,1)S(1)} %slice_bitcast_fusion), channel_id=1, source_target_pairs={{0,8},{8,16},{16,24},{24,32},{32,40},{40,48},{48,56},{56,64},{64,7... | collective-permute-start | bytes 393224 | tf_op jit(solution)/shard_map/ppermute | solution.py:203
  19.6 182.0 %copy-start = (f32[16]{0:T(128)S(1)}, f32[16]{0:T(128)}, u32[]{:S(2)}) copy-start(f32[16]{0:T(128)} %concatenate.9.level_ref) | copy-start | bytes 196
  203.3 21.1 %all-to-all-start.1 = ((bf16[32,64,128]{2,1,0:T(8,128)(2,1)}), bf16[32,64,128]{2,1,0:T(8,128)(2,1)S(1)}, u32[]{:S(2)}, u32[]{:S(2)}) async-start(bf16[32,64,128]{2,1,0:T(8,128)(2,1)} %scan.1), calls=%async_computation.1 | async-start | bytes 1048576 | tf_op jit(solution)/shard_map/all_to_all | solution.py:267
  224.4 0.8 copy-start.1
Sparse Core Ops, SparseCore 0:
  10.9 132.4 all-gather.1
